TPU v7x, 128 devices: a whole 4x4x4 slice. The times are simulated.
128 devices in a mesh: row: 8 (over z, core), col: 16 (over y, x).
Axes of the slice: x: 4, y: 4, z: 4, core: 2. Of those that a mesh axis runs over, the one named last changes fastest.
Arguments:
- amp_tiles: float32 [16, 32, 256, 256], P('row', 'col'), may hold values from -6 to 6
- int_tiles: float32 [32, 32, 256, 256], P('col', 'row'), may hold values from -0.125 to 0.125
- resid_init: float32 [16, 32, 256, 256], P('row', 'col'), may hold values from -6 to 6
- triples: int32 [8, 16, 3, 32], P('row', 'col'), may hold values from 0 to 1023, as said below
Outputs:
- resid_out: float32 [16, 32, 256, 256], P('row', 'col')
Inputs may be any that keep to these rules, and one draw needn't show every extreme that they name: Each triple names tiles (i, j), (j, k), (i, k) with one i, j, k. The amplitude tile of every triple on device (r, c) is one that device holds. For every device and every column index q, exactly 2 distinct residual tiles held at (r, q) are named by that device's triples, each by exactly one of that device's triples. No triple is listed twice; the order of triples on a device is arbitrary.
All inputs are finite; a program needn't handle non-finite values.
Results may differ from a plain program's by a relative error of at most 0.0001.
Values sent between devices are 32-bit elements; how exact they have to be, the bound alone decides.
No kernel may reach another device: no remote copies, remote signals or barrier semaphores. Data moves between devices by JAX's collectives and lax.ppermute only.
A program may use at most 128 MiB of HBM per device.

v0:
```python
import jax
import jax.numpy as jnp
from jax import lax
from jax.sharding import PartitionSpec as P


def on_device(amp_tiles, int_tiles, resid_init, triples):
    occ_blocks = amp_tiles.shape[0]
    vir_blocks = amp_tiles.shape[1]
    width = amp_tiles.shape[2]
    own_k = resid_init.shape[1]
    col_count = lax.axis_size("col")
    all_k = own_k * col_count
    all_j = vir_blocks * col_count
    row_place = lax.axis_index("row")
    col_place = lax.axis_index("col")
    listing = triples[0, 0]
    amp_ids = listing[0]
    int_ids = listing[1]
    res_ids = listing[2]
    amp_occ = amp_ids // all_j - row_place * occ_blocks
    amp_vir = amp_ids % all_j - col_place * vir_blocks
    int_vir = int_ids // all_k - col_place * vir_blocks
    int_col = int_ids % all_k
    res_occ = res_ids // all_k - row_place * occ_blocks
    res_col = res_ids % all_k
    amp_index = amp_occ * vir_blocks + amp_vir
    int_index = int_vir * all_k + int_col
    gathered = lax.all_gather(int_tiles, "row", axis=1, tiled=True)
    amp_flat = amp_tiles.reshape(-1, width, width)
    int_flat = gathered.reshape(-1, width, width)
    target = res_occ * all_k + res_col
    slots_total = occ_blocks * all_k
    block = 8

    def add_block(partial_value, pieces):
        amp_pick, int_pick, target_pick = pieces
        products = jnp.einsum(
            "bxy,byz->bxz",
            amp_flat[amp_pick],
            int_flat[int_pick],
            precision=lax.Precision.HIGHEST,
            preferred_element_type=jnp.float32,
        )
        return (partial_value.at[target_pick].add(products), None)

    start = jnp.zeros((slots_total, width, width), jnp.float32)
    pieces = (amp_index.reshape(-1, block), int_index.reshape(-1, block), target.reshape(-1, block))
    partial_value, _ = lax.scan(add_block, start, pieces)
    summed = lax.psum_scatter(
        partial_value.reshape(occ_blocks, all_k, width, width),
        "col",
        scatter_dimension=1,
        tiled=True,
    )
    return resid_init + summed


def solution(mesh):
    return jax.shard_map(
        on_device,
        mesh=mesh,
        in_specs=(
            P("row", "col", None, None),
            P("col", "row", None, None),
            P("row", "col", None, None),
            P("row", "col", None, None),
        ),
        out_specs=P("row", "col", None, None),
        check_vma=False,
    )
```

profile of v0, /device:TPU:1, one launch (start us, length us, event | category | flops | bytes accessed | tf_op | source)
XLA Modules:
  0.0 409.5 jit_solution(13803242583573978467)
XLA Ops:
  6.5 0.7 all-gather.2.cloned.1.call-update
  7.6 90.2 %all-gather.2.cloned.1.call-done = f32[2,32,256,256]{3,2,1,0:T(8,128)} async-done(((f32[2,4,256,256]{3,2,1,0:T(8,128)}), f32[2,32,256,256]{3,2,1,0:T(8,128)}) %all-gather.2.cloned.1.call-update) | async-done | bytes 16777232 | tf_op jit(solution)/shard_map/all_gather | solution.py:29
  97.9 7.8 %broadcast_in_dim.2 = f32[64,256,256]{2,1,0:T(8,128)} broadcast(f32[]{:T(128)} %constant.72.clone.1), dimensions={} | broadcast | bytes 16777220 | tf_op jit(solution)/shard_map/broadcast_in_dim | solution.py:47
  105.6 74.2 %while.10 = (s32[]{:T(128)}, f32[64,256,256]{2,1,0:T(8,128)}, s32[4,8]{1,0:T(4,128)S(1)}, s32[4,8]{1,0:T(4,128)S(1)}, f32[4,256,256]{2,1,0:T(8,128)S(1)}, /*inde...) while((s32[]{:T(128)}, f32[64,256,256]{2,1,0:T(8,128)}, s32[4,8]{1,0:T(4,128)S(1)}, ...), condition=%wide.region_2.3_spmd, body=%wide.region_0.2_spmd.sunk | while | flops 1611139200 | bytes 20980156 | solution.py:49
  105.7 2.0 gather_fusion
  107.7 7.8 %gather_fusion.1 = f32[8,256,256]{2,1,0:T(8,128)} fusion(f32[64,256,256]{2,1,0:T(8,128)} %get-tuple-element.133, s32[1024]{0:T(1024)S(1)} %pad_clamp_fusion.5), kind=kCustom, calls=%fused_computation.1.clone.1 | custom fusion | bytes 4194336 | tf_op jit(solution)/shard_map/while/body/eval_jaxpr/gather | solution.py:41
  115.5 4.3 %fusion.34 = f32[8,256,256]{2,1,0:T(8,128)S(1)} fusion(f32[8,256,256]{2,1,0:T(8,128)} %gather_fusion, f32[8,256,256]{2,1,0:T(8,128)} %gather_fusion.1), kind=kOutput, calls=%fused_computation.55.clone.1 | convolution fusion | flops 1610612736 | bytes 6291456 | tf_op jit(solution)/shard_map/while/body/eval_jaxpr/bxy,byz->bxz/dot_general | solution.py:38
  119.8 4.4 %scatter_fusion = f32[64,256,256]{2,1,0:T(8,128)} fusion(f32[64,256,256]{2,1,0:T(8,128)} %get-tuple-element.120, s32[8]{0:T(128)S(1)} %get-tuple-element.109, f32[8,256,256]{2,1,0:T(8,128)S(1)} %fusion.34), kind=kCustom, calls=%fused_computation.2.clone.1 | custom fusion | flops 524288 | bytes 6291488 | tf_op jit(solution)/shard_map/while/body/eval_jaxpr/scatter-add | solution.py:45
  124.2 2.0 gather_fusion
  126.2 7.8 %gather_fusion.1 = f32[8,256,256]{2,1,0:T(8,128)} fusion(f32[64,256,256]{2,1,0:T(8,128)} %get-tuple-element.133, s32[1024]{0:T(1024)S(1)} %pad_clamp_fusion.5), kind=kCustom, calls=%fused_computation.1.clone.1 | custom fusion | bytes 4194336 | tf_op jit(solution)/shard_map/while/body/eval_jaxpr/gather | solution.py:41
  134.0 4.3 %fusion.34 = f32[8,256,256]{2,1,0:T(8,128)S(1)} fusion(f32[8,256,256]{2,1,0:T(8,128)} %gather_fusion, f32[8,256,256]{2,1,0:T(8,128)} %gather_fusion.1), kind=kOutput, calls=%fused_computation.55.clone.1 | convolution fusion | flops 1610612736 | bytes 6291456 | tf_op jit(solution)/shard_map/while/body/eval_jaxpr/bxy,byz->bxz/dot_general | solution.py:38
  138.3 4.4 %scatter_fusion = f32[64,256,256]{2,1,0:T(8,128)} fusion(f32[64,256,256]{2,1,0:T(8,128)} %get-tuple-element.120, s32[8]{0:T(128)S(1)} %get-tuple-element.109, f32[8,256,256]{2,1,0:T(8,128)S(1)} %fusion.34), kind=kCustom, calls=%fused_computation.2.clone.1 | custom fusion | flops 524288 | bytes 6291488 | tf_op jit(solution)/shard_map/while/body/eval_jaxpr/scatter-add | solution.py:45
  142.8 2.0 gather_fusion
  144.8 7.8 %gather_fusion.1 = f32[8,256,256]{2,1,0:T(8,128)} fusion(f32[64,256,256]{2,1,0:T(8,128)} %get-tuple-element.133, s32[1024]{0:T(1024)S(1)} %pad_clamp_fusion.5), kind=kCustom, calls=%fused_computation.1.clone.1 | custom fusion | bytes 4194336 | tf_op jit(solution)/shard_map/while/body/eval_jaxpr/gather | solution.py:41
  152.6 4.3 %fusion.34 = f32[8,256,256]{2,1,0:T(8,128)S(1)} fusion(f32[8,256,256]{2,1,0:T(8,128)} %gather_fusion, f32[8,256,256]{2,1,0:T(8,128)} %gather_fusion.1), kind=kOutput, calls=%fused_computation.55.clone.1 | convolution fusion | flops 1610612736 | bytes 6291456 | tf_op jit(solution)/shard_map/while/body/eval_jaxpr/bxy,byz->bxz/dot_general | solution.py:38
  156.9 4.4 %scatter_fusion = f32[64,256,256]{2,1,0:T(8,128)} fusion(f32[64,256,256]{2,1,0:T(8,128)} %get-tuple-element.120, s32[8]{0:T(128)S(1)} %get-tuple-element.109, f32[8,256,256]{2,1,0:T(8,128)S(1)} %fusion.34), kind=kCustom, calls=%fused_computation.2.clone.1 | custom fusion | flops 524288 | bytes 6291488 | tf_op jit(solution)/shard_map/while/body/eval_jaxpr/scatter-add | solution.py:45
  161.3 2.0 gather_fusion
  163.3 7.8 %gather_fusion.1 = f32[8,256,256]{2,1,0:T(8,128)} fusion(f32[64,256,256]{2,1,0:T(8,128)} %get-tuple-element.133, s32[1024]{0:T(1024)S(1)} %pad_clamp_fusion.5), kind=kCustom, calls=%fused_computation.1.clone.1 | custom fusion | bytes 4194336 | tf_op jit(solution)/shard_map/while/body/eval_jaxpr/gather | solution.py:41
  171.2 4.3 %fusion.34 = f32[8,256,256]{2,1,0:T(8,128)S(1)} fusion(f32[8,256,256]{2,1,0:T(8,128)} %gather_fusion, f32[8,256,256]{2,1,0:T(8,128)} %gather_fusion.1), kind=kOutput, calls=%fused_computation.55.clone.1 | convolution fusion | flops 1610612736 | bytes 6291456 | tf_op jit(solution)/shard_map/while/body/eval_jaxpr/bxy,byz->bxz/dot_general | solution.py:38
  175.5 4.4 %scatter_fusion = f32[64,256,256]{2,1,0:T(8,128)} fusion(f32[64,256,256]{2,1,0:T(8,128)} %get-tuple-element.120, s32[8]{0:T(128)S(1)} %get-tuple-element.109, f32[8,256,256]{2,1,0:T(8,128)S(1)} %fusion.34), kind=kCustom, calls=%fused_computation.2.clone.1 | custom fusion | flops 524288 | bytes 6291488 | tf_op jit(solution)/shard_map/while/body/eval_jaxpr/scatter-add | solution.py:45
  179.9 0.6 copy-done.3
  180.5 0.6 dynamic-slice
  181.7 218.7 %all-reduce.3.cloned.1.call-done = f32[2,32,256,256]{3,2,1,0:T(8,128)} async-done(((f32[2,32,256,256]{3,2,1,0:T(8,128)}), f32[2,32,256,256]{3,2,1,0:T(8,128)}) %all-reduce.3.cloned.1.call-update) | async-done | bytes 16777232
  400.4 2.3 dynamic-slice_add_fusion
  (32 shorter events, 0.5 us)
Async XLA Ops:
  6.5 0.8 copy-start.2
  6.5 91.3 %all-gather.2.cloned.1.call-start = ((), (), s32[]{:S(2)}) async-start(), calls=%async_computation | async-start | bytes 18874368 | tf_op jit(solution)/shard_map/all_gather | solution.py:29
  7.3 393.1 %all-reduce.3.cloned.1.call-start = ((), (), s32[]{:S(2)}) async-start(), calls=%async_computation.1 | async-start | bytes 33554432
  97.9 7.8 %copy-start = (f32[2,2,256,256]{3,2,1,0:T(8,128)S(1)}, f32[2,2,256,256]{3,2,1,0:T(8,128)}, u32[]{:S(2)}) copy-start(f32[2,2,256,256]{3,2,1,0:T(8,128)} %param.6) | copy-start | bytes 3145732
  179.8 0.7 copy-start.3
  179.8 220.5 %copy-start.1 = (f32[2,2,256,256]{3,2,1,0:T(8,128)S(1)}, f32[2,2,256,256]{3,2,1,0:T(8,128)}, u32[]{:S(2)}) copy-start(f32[2,2,256,256]{3,2,1,0:T(8,128)} %param.8) | copy-start | bytes 3145732
Sparse Core Ops, SparseCore 0:
  9.1 88.7 all-gather.1
  180.0 220.3 all-reduce.2
where the time goes:
time: 410 us
  waiting for transfers between devices  310 us (76%)
  local copies, waits for them, and re-layouts  48.5 us (12%)
  other arithmetic  20 us (5%)
  matrix products  17.2 us (4%)
  between operations  14.1 us (3%)
    unnamed x3, waiting for transfers between devices  219 us
    all_gather x1, waiting for transfers between devices, on_device(): gathered = lax.all_gather(int_tiles, 'row', axis=1, tiled=True)  90.2 us
    gather x4, local copies, waits for them, and re-layouts, add_block(): int_flat[int_pick]  31.3 us
    scatter-add x4, other arithmetic, add_block(): return (partial_value.at[target_pick].add(products), None)  17.5 us
    dot_general x4, matrix products, add_block(): jnp.einsum('bxy,byz->bxz', amp_flat[amp_pick], int_flat[int_pick], precis...  17.2 us
  transfers between devices with their start and end apart: 2, of which 2 were waited for; matrix products, arithmetic and copies ran while one was open for 0% of the time, Pallas kernels for 0%

commit v1 on v0

--- a/solution.py
+++ b/solution.py
@@ -26,7 +26,9 @@
     res_col = res_ids % all_k
     amp_index = amp_occ * vir_blocks + amp_vir
     int_index = int_vir * all_k + int_col
-    gathered = lax.all_gather(int_tiles, "row", axis=1, tiled=True)
+    gathered = jnp.concatenate(
+        lax.all_to_all(jnp.stack([int_tiles] * lax.axis_size("row")), "row", 0, 0), axis=1
+    )
     amp_flat = amp_tiles.reshape(-1, width, width)
     int_flat = gathered.reshape(-1, width, width)
     target = res_occ * all_k + res_col

time: 410 us -> 530 us (1.29)
  waiting for transfers between devices: 310 us -> 402 us
  local copies, waits for them, and re-layouts: 48.5 us -> 69.4 us
  starting transfers between devices: 0.04 us -> 7.18 us
    all_to_all x0 -> x1, waiting for transfers between devices: none -> 183 us  [on_device(): lax.all_to_all(jnp.stack([int_tiles] * lax.axis_size('row')), 'row', 0, 0)]
    all_gather x1 -> x0, waiting for transfers between devices: 90.2 us -> none  [on_device(): gathered = lax.all_gather(int_tiles, 'row', axis=1, tiled=True)]
    all_to_all x0 -> x1, local copies, waits for them, and re-layouts: none -> 11.5 us  [on_device(): lax.all_to_all(jnp.stack([int_tiles] * lax.axis_size('row')), 'row', 0, 0)]
    another operation x0 -> x1, local copies, waits for them, and re-layouts: none -> 9.48 us  [on_device(): jnp.stack([int_tiles] * lax.axis_size('row'))]
    all_to_all x0 -> x1, starting transfers between devices: none -> 7.18 us  [on_device(): lax.all_to_all(jnp.stack([int_tiles] * lax.axis_size('row')), 'row', 0, 0)]
    unnamed x3 -> x2, waiting for transfers between devices: 219 us -> 219 us
where the time goes in v1:
time: 530 us
  waiting for transfers between devices  402 us (76%)
  local copies, waits for them, and re-layouts  69.4 us (13%)
  other arithmetic  20 us (4%)
  matrix products  17.2 us (3%)
  between operations  14.1 us (3%)
  starting transfers between devices  7.18 us (1%)
    unnamed x2, waiting for transfers between devices  219 us
    all_to_all x1, waiting for transfers between devices, on_device(): lax.all_to_all(jnp.stack([int_tiles] * lax.axis_size('row')), 'row', 0, 0)  183 us
    gather x4, local copies, waits for them, and re-layouts, add_block(): int_flat[int_pick]  31.3 us
    scatter-add x4, other arithmetic, add_block(): return (partial_value.at[target_pick].add(products), None)  17.5 us
    dot_general x4, matrix products, add_block(): jnp.einsum('bxy,byz->bxz', amp_flat[amp_pick], int_flat[int_pick], precis...  17.2 us
    all_to_all x1, local copies, waits for them, and re-layouts, on_device(): lax.all_to_all(jnp.stack([int_tiles] * lax.axis_size('row')), 'row', 0, 0)  11.5 us
  transfers between devices with their start and end apart: 2, of which 2 were waited for; matrix products, arithmetic and copies ran while one was open for 0% of the time, Pallas kernels for 0%

profile of v1, /device:TPU:1, one launch (start us, length us, event | category | flops | bytes accessed | tf_op | source)
XLA Modules:
  0.0 529.7 jit_solution(15877022099210956440)
XLA Ops:
  6.5 9.5 %stack.2 = f32[8,2,4,256,256]{4,3,2,1,0:T(8,128)} broadcast(f32[2,4,256,256]{3,2,1,0:T(8,128)} %param.7), dimensions={1,2,3,4} | broadcast | bytes 18874368 | tf_op jit(solution)/shard_map/stack | solution.py:30
  16.0 7.2 %all-to-all-start = ((f32[8,2,4,256,256]{4,3,2,1,0:T(8,128)}), f32[8,2,4,256,256]{4,3,2,1,0:T(8,128)}, u32[]{:S(2)}, u32[]{:S(2)}) async-start(f32[8,2,4,256,256]{4,3,2,1,0:T(8,128)} %stack.2), calls=%async_computation | async-start | bytes 33554432 | tf_op jit(solution)/shard_map/all_to_all | solution.py:30
  23.5 183.0 %all-to-all-done = f32[8,2,4,256,256]{4,3,2,1,0:T(8,128)} async-done(((f32[8,2,4,256,256]{4,3,2,1,0:T(8,128)}), f32[8,2,4,256,256]{4,3,2,1,0:T(8,128)}, u32[]{:S(2)}, u32[]{:S(2)}) %all-to-all-start) | async-done | bytes 16777248 | tf_op jit(solution)/shard_map/all_to_all | solution.py:30
  206.5 11.5 %copy.5 = f32[8,2,4,256,256]{4,3,2,0,1:T(8,128)} copy(f32[8,2,4,256,256]{4,3,2,1,0:T(8,128)} %all-to-all-done) | data formatting | bytes 33554432 | tf_op jit(solution)/shard_map/all_to_all | solution.py:30
  218.0 7.8 %broadcast_in_dim.2 = f32[64,256,256]{2,1,0:T(8,128)} broadcast(f32[]{:T(128)} %constant.72.clone.1), dimensions={} | broadcast | bytes 16777220 | tf_op jit(solution)/shard_map/broadcast_in_dim | solution.py:49
  225.8 74.2 %while.10 = (s32[]{:T(128)}, f32[64,256,256]{2,1,0:T(8,128)}, s32[4,8]{1,0:T(4,128)S(1)}, s32[4,8]{1,0:T(4,128)S(1)}, f32[4,256,256]{2,1,0:T(8,128)S(1)}, /*inde...) while((s32[]{:T(128)}, f32[64,256,256]{2,1,0:T(8,128)}, s32[4,8]{1,0:T(4,128)S(1)}, ...), condition=%wide.region_2.3_spmd, body=%wide.region_0.2_spmd.sunk | while | flops 1611139200 | bytes 20980156 | solution.py:51
  225.8 2.0 gather_fusion
  227.8 7.8 %gather_fusion.1 = f32[8,256,256]{2,1,0:T(8,128)} fusion(f32[64,256,256]{2,1,0:T(8,128)} %get-tuple-element.133, s32[1024]{0:T(1024)S(1)} %pad_clamp_fusion.5), kind=kCustom, calls=%fused_computation.1.clone.1 | custom fusion | bytes 4194336 | tf_op jit(solution)/shard_map/while/body/eval_jaxpr/gather | solution.py:43
  235.6 4.3 fusion.34
  240.0 4.4 scatter_fusion
  244.4 2.0 gather_fusion
  246.4 7.8 %gather_fusion.1 = f32[8,256,256]{2,1,0:T(8,128)} fusion(f32[64,256,256]{2,1,0:T(8,128)} %get-tuple-element.133, s32[1024]{0:T(1024)S(1)} %pad_clamp_fusion.5), kind=kCustom, calls=%fused_computation.1.clone.1 | custom fusion | bytes 4194336 | tf_op jit(solution)/shard_map/while/body/eval_jaxpr/gather | solution.py:43
  254.2 4.3 fusion.34
  258.5 4.4 scatter_fusion
  263.0 2.0 gather_fusion
  265.0 7.8 %gather_fusion.1 = f32[8,256,256]{2,1,0:T(8,128)} fusion(f32[64,256,256]{2,1,0:T(8,128)} %get-tuple-element.133, s32[1024]{0:T(1024)S(1)} %pad_clamp_fusion.5), kind=kCustom, calls=%fused_computation.1.clone.1 | custom fusion | bytes 4194336 | tf_op jit(solution)/shard_map/while/body/eval_jaxpr/gather | solution.py:43
  272.8 4.3 fusion.34
  277.1 4.4 scatter_fusion
  281.5 2.0 gather_fusion
  283.5 7.8 %gather_fusion.1 = f32[8,256,256]{2,1,0:T(8,128)} fusion(f32[64,256,256]{2,1,0:T(8,128)} %get-tuple-element.133, s32[1024]{0:T(1024)S(1)} %pad_clamp_fusion.5), kind=kCustom, calls=%fused_computation.1.clone.1 | custom fusion | bytes 4194336 | tf_op jit(solution)/shard_map/while/body/eval_jaxpr/gather | solution.py:43
  291.3 4.3 fusion.34
  295.6 4.4 scatter_fusion
  301.9 218.6 %all-reduce.3.cloned.1.call-done = f32[2,32,256,256]{3,2,1,0:T(8,128)} async-done(((f32[2,32,256,256]{3,2,1,0:T(8,128)}), f32[2,32,256,256]{3,2,1,0:T(8,128)}) %all-reduce.3.cloned.1.call-update) | async-done | bytes 16777232
  520.5 2.3 dynamic-slice_add_fusion
  (33 shorter events, 1.7 us)
Async XLA Ops:
  16.0 7.2 %copy-start.2 = (s32[1,1,3,32]{3,1,2,0:T(1,128)S(1)}, s32[1,1,3,32]{3,1,2,0:T(1,128)}, u32[]{:S(2)}) copy-start(s32[1,1,3,32]{3,1,2,0:T(1,128)} %param.9) | copy-start | bytes 1156
  16.0 190.5 %all-to-all-start = ((f32[8,2,4,256,256]{4,3,2,1,0:T(8,128)}), f32[8,2,4,256,256]{4,3,2,1,0:T(8,128)}, u32[]{:S(2)}, u32[]{:S(2)}) async-start(f32[8,2,4,256,256]{4,3,2,1,0:T(8,128)} %stack.2), calls=%async_computation | async-start | bytes 33554432 | tf_op jit(solution)/shard_map/all_to_all | solution.py:30
  23.2 497.3 %all-reduce.3.cloned.1.call-start = ((), (), s32[]{:S(2)}) async-start(), calls=%async_computation.1 | async-start | bytes 33554432
  218.0 7.8 %copy-start = (f32[2,2,256,256]{3,2,1,0:T(8,128)S(1)}, f32[2,2,256,256]{3,2,1,0:T(8,128)}, u32[]{:S(2)}) copy-start(f32[2,2,256,256]{3,2,1,0:T(8,128)} %param.6) | copy-start | bytes 3145732
  300.0 0.7 copy-start.3
  300.0 220.5 %copy-start.1 = (f32[2,2,256,256]{3,2,1,0:T(8,128)S(1)}, f32[2,2,256,256]{3,2,1,0:T(8,128)}, u32[]{:S(2)}) copy-start(f32[2,2,256,256]{3,2,1,0:T(8,128)} %param.8) | copy-start | bytes 3145732
Sparse Core Ops, SparseCore 0:
  300.1 220.3 all-reduce.2
